TPU v7x, 128 devices: a whole 4x4x4 slice. The times are simulated.
128 devices in a mesh: fsdp: 16 (over x_lo, y, core), tp: 8 (over x_hi, z).
Axes of the slice: x: 4 (x_hi: 2, x_lo: 2; x = x_hi * 2 + x_lo), y: 4, z: 4, core: 2. Of those that a mesh axis runs over, the one named last changes fastest.
Arguments:
- tokens: bfloat16 [16384, 2048], P(('fsdp', 'tp')), may hold values from -6 to 6
- grad_out: bfloat16 [16384, 2048], P(('fsdp', 'tp')), may hold values from -6 to 6
- adapter_ids: int32 [16], P('fsdp'), may hold values from 0 to 7
- first_gain: float32 [2048], replicated, may hold values from 0.1 to 1.9
- first_shift: float32 [2048], replicated, may hold values from -4 to 4
- joined_weight: bfloat16 [2048, 6144], P('fsdp', 'tp'), may hold values from -0.125 to 0.125
- joined_bias: float32 [6144], P('tp'), may hold values from -4 to 4
- dense_weight: bfloat16 [2048, 2048], P('tp', 'fsdp'), may hold values from -0.5 to 0.5
- dense_bias: float32 [2048], replicated, may hold values from -4 to 4
- second_gain: float32 [2048], replicated, may hold values from 0.1 to 1.9
- second_shift: float32 [2048], replicated, may hold values from -4 to 4
- up_weight: bfloat16 [2048, 8192], P('fsdp', 'tp'), may hold values from -0.125 to 0.125
- up_bias: float32 [8192], P('tp'), may hold values from -6 to 6
- down_weight: bfloat16 [8192, 2048], P('tp', 'fsdp'), may hold values from -0.125 to 0.125
- down_bias: float32 [2048], replicated, may hold values from -4 to 4
- joined_adapt_in: bfloat16 [8, 2048, 16], replicated, may hold values from -0.125 to 0.125
- joined_adapt_out: bfloat16 [8, 16, 6144], P(None, None, 'tp'), may hold values from -2 to 2
- dense_adapt_in: bfloat16 [8, 2048, 16], P(None, 'tp'), may hold values from -0.5 to 0.5
- dense_adapt_out: bfloat16 [8, 16, 2048], replicated, may hold values from -2 to 2
- up_adapt_in: bfloat16 [8, 2048, 16], replicated, may hold values from -0.125 to 0.125
- up_adapt_out: bfloat16 [8, 16, 8192], P(None, None, 'tp'), may hold values from -2 to 2
- down_adapt_in: bfloat16 [8, 8192, 16], P(None, 'tp'), may hold values from -0.125 to 0.125
- down_adapt_out: bfloat16 [8, 16, 2048], replicated, may hold values from -2 to 2
Outputs:
- layer_out: bfloat16 [16384, 2048], P(('fsdp', 'tp'))
- grad_tokens: float32 [16384, 2048], P(('fsdp', 'tp'))
- grad_joined_in: float32 [8, 2048, 16], replicated
- grad_joined_out: float32 [8, 16, 6144], P(None, None, 'tp')
- grad_dense_in: float32 [8, 2048, 16], P(None, 'tp')
- grad_dense_out: float32 [8, 16, 2048], replicated
- grad_up_in: float32 [8, 2048, 16], replicated
- grad_up_out: float32 [8, 16, 8192], P(None, None, 'tp')
- grad_down_in: float32 [8, 8192, 16], P(None, 'tp')
- grad_down_out: float32 [8, 16, 2048], replicated
All inputs are finite; a program needn't handle non-finite values.
Results may differ from a plain program's by a relative error of at most 0.02.
Values may be sent and summed in bfloat16 or wider, within the bound.
A program may use at most 128 MiB of HBM per device.

v0:
```python
import jax
import jax.numpy as jnp
from jax import lax
from jax.sharding import PartitionSpec as P

HEADS = 32
HEAD_DIM = 64
EPSILON = 1e-05
MASKED = -1e30
HIGHEST = lax.Precision.HIGHEST


def split_up(value, dim, size):
    before, after = (value.shape[:dim], value.shape[dim + 1 :])
    return jnp.moveaxis(value.reshape(*before, size, -1, *after), dim, 0)


def sum_at_owner(value, axis, dim):
    blocks = split_up(value, dim, lax.axis_size(axis))
    arrived = lax.all_to_all(blocks, axis, split_axis=0, concat_axis=0, tiled=True)
    return arrived.astype(jnp.float32).sum(axis=0)


def together(arrays, axis):
    ends = [0]
    for a in arrays:
        ends.append(ends[-1] + a.size)
    so_far = lax.psum(jnp.concatenate([a.ravel() for a in arrays]), axis)
    return tuple((so_far[b:e].reshape(a.shape) for a, b, e in zip(arrays, ends, ends[1:])))


def layer_norm(rows_in, gain, shift):
    row_mean = jnp.mean(rows_in, axis=-1, keepdims=True)
    centered = rows_in - row_mean
    variance = jnp.mean(centered * centered, axis=-1, keepdims=True)
    return centered * lax.rsqrt(variance + EPSILON) * gain + shift


def exact_gelu(values_in):
    return jax.nn.gelu(values_in, approximate=False)


def choose(onehot, tensor_in):
    return jnp.einsum(
        "sa,a...->s...", onehot, tensor_in, preferred_element_type=jnp.float32
    ).astype(jnp.bfloat16)


def spread(onehot, grads_in):
    return jnp.einsum("sa,s...->a...", onehot, grads_in, precision=HIGHEST)


def seq_dot(left_side, right_side):
    return jnp.einsum("slk,skn->sln", left_side, right_side, preferred_element_type=jnp.float32)


def seq_dot_back(left_side, right_side):
    return jnp.einsum("sln,skn->slk", left_side, right_side, preferred_element_type=jnp.float32)


def seq_outer(left_side, right_side):
    return jnp.einsum("slk,sln->skn", left_side, right_side, preferred_element_type=jnp.float32)


def dot_back(left_side, right_side):
    return lax.dot_general(
        left_side, right_side, (((1,), (1,)), ((), ())), preferred_element_type=jnp.float32
    )


def widen_rows(low_rows):
    seq_total = low_rows.shape[0]
    identity = jnp.eye(seq_total, dtype=low_rows.dtype)
    widened = jnp.einsum("slr,st->sltr", low_rows, identity)
    return widened.reshape(seq_total * low_rows.shape[1], seq_total * low_rows.shape[2])


def block_scores(queries, keys_all, slopes, offset, block_rows):
    length = keys_all.shape[0]
    row_ids = offset + jnp.arange(block_rows)
    distance = (row_ids[:, None] - jnp.arange(length)[None, :]).astype(jnp.float32)
    query_block = lax.dynamic_slice_in_dim(queries, offset, block_rows, 0)
    raw_scores = jnp.einsum(
        "qhe,khe->hqk", query_block, keys_all, preferred_element_type=jnp.float32
    )
    scaled = (raw_scores - slopes[:, None, None] * distance[None]) * 0.125
    return (jnp.where(distance[None] >= 0, scaled, MASKED), query_block)


def attend(queries, keys_all, values_all, slopes, block_rows):
    length = queries.shape[0]

    def one_block(block_index):
        scores, _ = block_scores(queries, keys_all, slopes, block_index * block_rows, block_rows)
        row_max = jnp.max(scores, axis=-1, keepdims=True)
        exp_scores = jnp.exp(scores - row_max)
        row_sum = jnp.sum(exp_scores, axis=-1, keepdims=True)
        attn_probs = (exp_scores / row_sum).astype(jnp.bfloat16)
        context = jnp.einsum(
            "hqk,khe->qhe", attn_probs, values_all, preferred_element_type=jnp.float32
        )
        return (context.astype(jnp.bfloat16), (row_max + jnp.log(row_sum))[..., 0])

    context, log_sums = lax.map(one_block, jnp.arange(length // block_rows))
    return (context.reshape(queries.shape), log_sums)


def attend_back(queries, keys_all, values_all, grad_context, log_sums, slopes, block_rows):
    length = queries.shape[0]

    def one_block(running, block_index):
        grad_keys, grad_values = running
        offset = block_index * block_rows
        scores, query_block = block_scores(queries, keys_all, slopes, offset, block_rows)
        grad_block = lax.dynamic_slice_in_dim(grad_context, offset, block_rows, 0)
        attn_probs = jnp.exp(scores - log_sums[block_index][:, :, None])
        grad_probs = jnp.einsum(
            "qhe,khe->hqk", grad_block, values_all, preferred_element_type=jnp.float32
        )
        row_dot = jnp.sum(attn_probs * grad_probs, axis=-1, keepdims=True)
        grad_scores = (attn_probs * (grad_probs - row_dot)).astype(jnp.bfloat16)
        grad_queries = (
            jnp.einsum("hqk,khe->qhe", grad_scores, keys_all, preferred_element_type=jnp.float32)
            * 0.125
        )
        grad_keys = (
            grad_keys
            + jnp.einsum(
                "hqk,qhe->khe", grad_scores, query_block, preferred_element_type=jnp.float32
            )
            * 0.125
        )
        grad_values = grad_values + jnp.einsum(
            "hqk,qhe->khe",
            attn_probs.astype(jnp.bfloat16),
            grad_block,
            preferred_element_type=jnp.float32,
        )
        return ((grad_keys, grad_values), grad_queries)

    zeros_kv = jnp.zeros(keys_all.shape, jnp.float32)
    (grad_keys, grad_values), grad_queries = lax.scan(
        one_block, (zeros_kv, zeros_kv), jnp.arange(length // block_rows)
    )
    return (grad_queries.reshape(queries.shape), grad_keys, grad_values)


def local(
    tokens,
    grad_out,
    adapter_ids,
    first_gain,
    first_shift,
    joined_weight,
    joined_bias,
    dense_weight,
    dense_bias,
    second_gain,
    second_shift,
    up_weight,
    up_bias,
    down_weight,
    down_bias,
    joined_adapt_in,
    joined_adapt_out,
    dense_adapt_in,
    dense_adapt_out,
    up_adapt_in,
    up_adapt_out,
    down_adapt_in,
    down_adapt_out,
):
    local_rows = tokens.shape[0]
    model_width = tokens.shape[1]
    seq_total = adapter_ids.shape[0]
    group_rows = local_rows * lax.axis_size("tp")
    length = group_rows // seq_total
    block_rows = min(512, length)
    set_count = joined_adapt_in.shape[0]
    low_rank = joined_adapt_in.shape[2]
    joined_width = joined_bias.shape[0]
    hidden_width = up_bias.shape[0]
    local_heads = joined_width // (3 * HEAD_DIM)
    head_cols = local_heads * HEAD_DIM
    head_ids = lax.axis_index("tp") * local_heads + jnp.arange(local_heads)
    slopes = jnp.exp2(-8.0 * (head_ids + 1).astype(jnp.float32) / HEADS)
    matches = adapter_ids[:, None] == jnp.arange(set_count)[None, :]
    onehot_low = matches.astype(jnp.bfloat16)
    onehot_high = matches.astype(jnp.float32)
    pick_joined_in = choose(onehot_low, joined_adapt_in)
    pick_joined_out = choose(onehot_low, joined_adapt_out)
    pick_dense_in = choose(onehot_low, dense_adapt_in)
    pick_dense_out = choose(onehot_low, dense_adapt_out)
    pick_up_in = choose(onehot_low, up_adapt_in)
    pick_up_out = choose(onehot_low, up_adapt_out)
    pick_down_in = choose(onehot_low, down_adapt_in)
    pick_down_out = choose(onehot_low, down_adapt_out)
    residual_in = tokens.astype(jnp.float32)
    normed_one = layer_norm(residual_in, first_gain, first_shift).astype(jnp.bfloat16)
    gathered_one = lax.all_gather(normed_one, "tp", axis=0, tiled=True)
    w_joined, w_dense = (
        lax.all_gather(joined_weight, "fsdp", axis=0, tiled=True),
        lax.all_gather(dense_weight, "fsdp", axis=1, tiled=True),
    )
    seq_one = gathered_one.reshape(seq_total, length, model_width)
    low_joined = seq_dot(seq_one, pick_joined_in).astype(jnp.bfloat16)
    joined_cols = jnp.dot(gathered_one, w_joined, preferred_element_type=jnp.float32).reshape(
        seq_total, length, joined_width
    )
    joined_cols = (joined_cols + seq_dot(low_joined, pick_joined_out) + joined_bias).astype(
        jnp.bfloat16
    )
    joined_heads = joined_cols.reshape(seq_total, length, local_heads, 3, HEAD_DIM)
    sequence = 0
    context, log_sums = attend(
        joined_heads[sequence, :, :, 0, :],
        joined_heads[sequence, :, :, 1, :],
        joined_heads[sequence, :, :, 2, :],
        slopes,
        block_rows,
    )
    contexts = [context]
    log_list = [log_sums]
    seq_context = jnp.stack(contexts).reshape(seq_total, length, head_cols)
    context_rows = seq_context.reshape(group_rows, head_cols)
    low_dense = seq_dot(seq_context, pick_dense_in).astype(jnp.bfloat16)
    wide_dense = widen_rows(low_dense)
    stack_dense = pick_dense_out.reshape(seq_total * low_rank, model_width)
    rows_low = wide_dense
    attn_sum = sum_at_owner(
        (
            jnp.dot(context_rows, w_dense, preferred_element_type=jnp.float32)
            + jnp.dot(rows_low, stack_dense, preferred_element_type=jnp.float32)
        ).astype(jnp.bfloat16),
        "tp",
        0,
    )
    residual_mid = residual_in + attn_sum + dense_bias
    normed_two = layer_norm(residual_mid, second_gain, second_shift).astype(jnp.bfloat16)
    gathered_two = lax.all_gather(normed_two, "tp", axis=0, tiled=True)
    w_up, w_down = (
        lax.all_gather(up_weight, "fsdp", axis=0, tiled=True),
        lax.all_gather(down_weight, "fsdp", axis=1, tiled=True),
    )
    seq_two = gathered_two.reshape(seq_total, length, model_width)
    low_up = seq_dot(seq_two, pick_up_in).astype(jnp.bfloat16)
    pre_act = (
        jnp.dot(gathered_two, w_up, preferred_element_type=jnp.float32)
        + seq_dot(low_up, pick_up_out).reshape(group_rows, hidden_width)
        + up_bias
    )
    activated = exact_gelu(pre_act).astype(jnp.bfloat16)
    seq_act = activated.reshape(seq_total, length, hidden_width)
    low_down = seq_dot(seq_act, pick_down_in).astype(jnp.bfloat16)
    wide_down = widen_rows(low_down)
    stack_down = pick_down_out.reshape(seq_total * low_rank, model_width)
    rows_low = wide_down
    mlp_sum = sum_at_owner(
        (
            jnp.dot(activated, w_down, preferred_element_type=jnp.float32)
            + jnp.dot(rows_low, stack_down, preferred_element_type=jnp.float32)
        ).astype(jnp.bfloat16),
        "tp",
        0,
    )
    layer_out = (residual_mid + mlp_sum + down_bias).astype(jnp.bfloat16)
    grad_mlp = lax.all_gather(grad_out, "tp", axis=0, tiled=True)
    back_up, back_down = (w_up, w_down)
    seq_grad_mlp = grad_mlp.reshape(seq_total, length, model_width)
    grad_low_down = seq_dot_back(seq_grad_mlp, pick_down_out).astype(jnp.bfloat16)
    term_down_out = seq_outer(low_down, seq_grad_mlp)
    term_down_in = seq_outer(seq_act, grad_low_down)
    grad_act = dot_back(grad_mlp, back_down) + seq_dot_back(grad_low_down, pick_down_in).reshape(
        group_rows, hidden_width
    )
    _, gelu_pull = jax.vjp(exact_gelu, pre_act)
    grad_pre = gelu_pull(grad_act)[0].astype(jnp.bfloat16)
    seq_grad_pre = grad_pre.reshape(seq_total, length, hidden_width)
    grad_low_up = seq_dot_back(seq_grad_pre, pick_up_out).astype(jnp.bfloat16)
    term_up_out = seq_outer(low_up, seq_grad_pre)
    term_up_in = seq_outer(seq_two, grad_low_up)
    wide_up = widen_rows(grad_low_up)
    stack_up = jnp.swapaxes(pick_up_in, 1, 2).reshape(seq_total * low_rank, model_width)
    rows_grad = grad_pre
    rows_low = wide_up
    grad_norm_two = sum_at_owner(
        (
            dot_back(rows_grad, back_up)
            + jnp.dot(rows_low, stack_up, preferred_element_type=jnp.float32)
        ).astype(jnp.bfloat16),
        "tp",
        0,
    )
    _, norm_pull_two = jax.vjp(
        lambda rows_in: layer_norm(rows_in, second_gain, second_shift), residual_mid
    )
    grad_mid = grad_out.astype(jnp.float32) + norm_pull_two(grad_norm_two)[0]
    grad_attn = lax.all_gather(grad_mid.astype(jnp.bfloat16), "tp", axis=0, tiled=True)
    back_joined, back_dense = (w_joined, w_dense)
    seq_grad_attn = grad_attn.reshape(seq_total, length, model_width)
    grad_low_dense = seq_dot_back(seq_grad_attn, pick_dense_out).astype(jnp.bfloat16)
    term_dense_out = seq_outer(low_dense, seq_grad_attn)
    term_dense_in = seq_outer(seq_context, grad_low_dense)
    grad_context = dot_back(grad_attn, back_dense) + seq_dot_back(
        grad_low_dense, pick_dense_in
    ).reshape(group_rows, head_cols)
    grad_context = grad_context.astype(jnp.bfloat16).reshape(
        seq_total, length, local_heads, HEAD_DIM
    )
    sequence = 0
    grad_query, grad_key, grad_value = attend_back(
        joined_heads[sequence, :, :, 0, :],
        joined_heads[sequence, :, :, 1, :],
        joined_heads[sequence, :, :, 2, :],
        grad_context[sequence],
        log_list[sequence],
        slopes,
        block_rows,
    )
    grad_parts = [jnp.stack((grad_query, grad_key, grad_value), axis=2)]
    grad_joined = (
        jnp.stack(grad_parts).astype(jnp.bfloat16).reshape(seq_total, length, joined_width)
    )
    grad_low_joined = seq_dot_back(grad_joined, pick_joined_out).astype(jnp.bfloat16)
    term_joined_out = seq_outer(low_joined, grad_joined)
    term_joined_in = seq_outer(seq_one, grad_low_joined)
    grad_joined_rows = grad_joined.reshape(group_rows, joined_width)
    wide_joined = widen_rows(grad_low_joined)
    stack_joined = jnp.swapaxes(pick_joined_in, 1, 2).reshape(seq_total * low_rank, model_width)
    rows_grad = grad_joined_rows
    rows_low = wide_joined
    grad_norm_one = sum_at_owner(
        (
            dot_back(rows_grad, back_joined)
            + jnp.dot(rows_low, stack_joined, preferred_element_type=jnp.float32)
        ).astype(jnp.bfloat16),
        "tp",
        0,
    )
    _, norm_pull_one = jax.vjp(
        lambda rows_in: layer_norm(rows_in, first_gain, first_shift), residual_in
    )
    grad_tokens = grad_mid + norm_pull_one(grad_norm_one)[0]
    wide_sums = tuple(
        (
            part.astype(jnp.float32)
            for part in together(
                (
                    spread(onehot_high, term_joined_out).astype(jnp.bfloat16),
                    spread(onehot_high, term_dense_in).astype(jnp.bfloat16),
                    spread(onehot_high, term_up_out).astype(jnp.bfloat16),
                    spread(onehot_high, term_down_in).astype(jnp.bfloat16),
                ),
                "fsdp",
            )
        )
    )
    both_sums = lax.psum(
        (
            spread(onehot_high, term_joined_in),
            spread(onehot_high, term_dense_out),
            spread(onehot_high, term_up_in),
            spread(onehot_high, term_down_out),
        ),
        ("fsdp", "tp"),
    )
    return (
        layer_out,
        grad_tokens,
        both_sums[0],
        wide_sums[0],
        wide_sums[1],
        both_sums[1],
        both_sums[2],
        wide_sums[2],
        wide_sums[3],
        both_sums[3],
    )


def solution(mesh):
    return jax.shard_map(
        local,
        mesh=mesh,
        in_specs=(
            P(("fsdp", "tp"), None),
            P(("fsdp", "tp"), None),
            P("fsdp"),
            P(),
            P(),
            P("fsdp", "tp"),
            P("tp"),
            P("tp", "fsdp"),
            P(),
            P(),
            P(),
            P("fsdp", "tp"),
            P("tp"),
            P("tp", "fsdp"),
            P(),
            P(),
            P(None, None, "tp"),
            P(None, "tp", None),
            P(),
            P(),
            P(None, None, "tp"),
            P(None, "tp", None),
            P(),
        ),
        out_specs=(
            P(("fsdp", "tp"), None),
            P(("fsdp", "tp"), None),
            P(),
            P(None, None, "tp"),
            P(None, "tp", None),
            P(),
            P(),
            P(None, None, "tp"),
            P(None, "tp", None),
            P(),
        ),
        check_vma=False,
    )
```

profile of v0, /device:TPU:1, one launch (start us, length us, event | category | flops | bytes accessed | tf_op | source)
XLA Modules:
  0.0 977.7 jit_solution(4659292120763606901)
XLA Ops:
  11.0 2.3 fusion.50
  19.2 68.6 %all-gather.9.cloned.1.call-done = bf16[1024,2048]{1,0:T(8,128)(2,1)} async-done(((bf16[128,2048]{1,0:T(8,128)(2,1)}), bf16[1024,2048]{1,0:T(8,128)(2,1)}) %all-gather.9.cloned.1.call-update) | async-done | bytes 4194320 | tf_op jit(solution)/shard_map/all_gather | solution.py:200
  87.8 3.4 convolution_convert_fusion.5
  91.2 32.7 %all-gather.11.cloned.1.call-done = bf16[2048,768]{1,0:T(8,128)(2,1)} async-done(((bf16[128,768]{1,0:T(8,128)(2,1)}), bf16[2048,768]{1,0:T(8,128)(2,1)}) %all-gather.11.cloned.1.call-update) | async-done | bytes 3145744 | tf_op jit(solution)/shard_map/all_gather | solution.py:202
  123.9 6.4 fusion.96
  131.2 22.1 %while.28 = (s32[]{:T(128)}, bf16[2,512,4,64]{1,3,2,0:T(8,128)(2,1)S(1)}, f32[2,4,512]{2,1,0:T(4,128)S(1)}, s32[2]{0:T(128)S(1)}, bf16[1024,4,64]{0,2,1:T(8,128)...) while((s32[]{:T(128)}, ...), condition=%wide.region_5.6_spmd.clone, body=%wide.region_2.5_spmd.clone.sunk | while | flops 577370624 | bytes 37297388 | solution.py:104
  133.2 2.7 fusion.187
  135.9 2.9 fusion.188
  138.8 3.4 fusion.189
  144.2 2.7 fusion.187
  146.9 2.9 fusion.188
  149.9 3.4 fusion.189
  154.2 5.4 all-gather.13.cloned.1.call-done
  159.6 2.5 fusion.97
  163.4 62.2 %all_to_all.20 = bf16[8,128,2048]{2,1,0:T(8,128)(2,1)S(1)} all-to-all(bf16[8,128,2048]{2,1,0:T(8,128)(2,1)S(1)} %bitcast.233), channel_id=1, replica_groups=mesh['fsdp'=16,'tp'=8] {'tp'}, dimensions={0} | all-to-all | bytes 8388608 | tf_op jit(solution)/shard_map/all_to_all | solution.py:20
  230.5 1.5 fusion.56
  232.0 33.0 %all-gather.21.cloned.1.call-done = bf16[1024,2048]{1,0:T(8,128)(2,1)} async-done(((bf16[128,2048]{1,0:T(8,128)(2,1)}), bf16[1024,2048]{1,0:T(8,128)(2,1)}) %all-gather.21.cloned.1.call-update) | async-done | bytes 4194320 | tf_op jit(solution)/shard_map/all_gather | solution.py:267
  265.0 3.4 convolution_convert_fusion.3
  268.3 41.9 %all-gather.19.cloned.1.call-done = bf16[1024,2048]{1,0:T(8,128)(2,1)} async-done(((bf16[1024,128]{1,0:T(8,128)(2,1)}), bf16[1024,2048]{1,0:T(8,128)(2,1)}) %all-gather.19.cloned.1.call-update) | async-done | bytes 4194320 | tf_op jit(solution)/shard_map/all_gather | solution.py:243
  310.2 10.0 %fusion.100 = f32[1024,1024]{1,0:T(8,128)} fusion(bf16[1024,2048]{1,0:T(8,128)(2,1)} %all-gather.21.cloned.1.call-done, bf16[1024,2048]{1,0:T(8,128)(2,1)} %all-gather.19.cloned.1.call-done), kind=kOutput, calls=%fused_computation.187 | convolution fusion | flops 4294967296 | bytes 12582912 | tf_op jit(solution)/shard_map/dot_general | solution.py:66
  320.2 63.6 %all-gather.15.cloned.1.call-done = bf16[1024,2048]{1,0:T(8,128)(2,1)} async-done(((bf16[128,2048]{1,0:T(8,128)(2,1)}), bf16[1024,2048]{1,0:T(8,128)(2,1)}) %all-gather.15.cloned.1.call-update) | async-done | bytes 4194320 | tf_op jit(solution)/shard_map/all_gather | solution.py:240
  383.9 3.4 convolution_convert_fusion.4
  387.2 34.3 %all-gather.17.cloned.1.call-done = bf16[2048,1024]{1,0:T(8,128)(2,1)} async-done(((bf16[128,1024]{1,0:T(8,128)(2,1)}), bf16[2048,1024]{1,0:T(8,128)(2,1)}) %all-gather.17.cloned.1.call-update) | async-done | bytes 4194320 | tf_op jit(solution)/shard_map/all_gather | solution.py:242
  421.5 7.9 fusion.98
  429.5 11.2 %multiply_convert_fusion.2 = (bf16[1024,1024]{1,0:T(8,128)(2,1)}, f32[1024,1024]{1,0:T(8,128)S(1)}, f32[1024,1024]{1,0:T(8,128)S(1)}) fusion(f32[1024]{0:T(1024)S(1)} %copy-done.56, f32[1024,1024]{1,0:T(8,128)S(1)} %fusion.98, bf16[1024,16]{0,1:T(8,128)(2,1)S(1)} %convolution_convert_fusion.4, bf16[1,16,1024]{2,0,1:T(2,128)(2,1)S(1)} %fusion.66), kind=kOutput, calls=%fused_computation.60 | convolution fusion | flops 103809024 | bytes 14749696 | tf_op jit(solution)/shard_map/slk,skn->sln/dot_general | solution.py:54
  440.6 2.3 add_convert_fusion.4
  443.6 4.6 fusion.101
  448.2 3.3 add_convert_fusion.1
  451.5 6.5 all-to-all-start.2
  458.0 2.2 convolution_convert_fusion.6
  460.2 6.9 fusion.99
  467.2 3.4 add_convert_fusion.2
  470.5 36.2 %all-to-all-done.2 = bf16[8,128,2048]{2,1,0:T(8,128)(2,1)} async-done(((bf16[8,128,2048]{2,1,0:T(8,128)(2,1)}), bf16[8,128,2048]{2,1,0:T(8,128)(2,1)}, u32[]{:S(2)}, u32[]{:S(2)}) %all-to-all-start.2) | async-done | bytes 4194336 | tf_op jit(solution)/shard_map/all_to_all | solution.py:20
  506.8 5.1 all-to-all-start.1
  511.9 3.0 convert_reduce_fusion.1
  515.2 45.4 %all-to-all-done.1 = bf16[8,128,2048]{2,1,0:T(8,128)(2,1)} async-done(((bf16[8,128,2048]{2,1,0:T(8,128)(2,1)}), bf16[8,128,2048]{2,1,0:T(8,128)(2,1)}, u32[]{:S(2)}, u32[]{:S(2)}) %all-to-all-start.1) | async-done | bytes 4194336 | tf_op jit(solution)/shard_map/all_to_all | solution.py:20
  560.6 3.0 convert_reduce_fusion.2
  566.9 2.0 fusion.106
  569.8 2.3 fusion.107
  572.1 1.8 multiply_convert_fusion.1
  573.9 3.0 reshape.539
  576.9 3.7 fusion.109
  581.9 55.0 %all-gather.23.cloned.1.call-done = bf16[1024,2048]{1,0:T(8,128)(2,1)} async-done(((bf16[128,2048]{1,0:T(8,128)(2,1)}), bf16[1024,2048]{1,0:T(8,128)(2,1)}) %all-gather.23.cloned.1.call-update) | async-done | bytes 4194320 | tf_op jit(solution)/shard_map/all_gather | solution.py:298
  636.9 3.5 convolution_convert_fusion.1
  643.7 29.9 %while.29 = (s32[]{:T(128)}, f32[1024,4,64]{0,2,1:T(8,128)S(1)}, f32[1024,4,64]{0,2,1:T(8,128)S(1)}, bf16[2,512,4,64]{1,3,2,0:T(8,128)(2,1)}, s32[2]{0:T(128)S(1...) while((s32[]{:T(128)}, f32[1024,4,64]{0,2,1:T(8,128)S(1)}, ...), condition=%wide.region_15.16_spmd.clone, body=%wide.region_13.15_spmd.clone.sunk | while | flops 1369307648 | bytes 81836928 | solution.py:142
  647.8 2.4 fusion.199
  650.3 3.9 multiply_reduce_fusion.4
  662.6 2.4 fusion.199
  665.0 3.9 multiply_reduce_fusion.4
  673.7 1.6 copy.42
  679.0 5.4 fusion.103
  684.5 3.2 add_convert_fusion
  687.7 4.6 all-to-all-start.3
  692.3 3.0 fusion.110
  695.4 1.6 broadcast_multiply_fusion.1
  697.6 1.7 broadcast_multiply_fusion
  699.3 101.2 %all-reduce.4.cloned.1.call-done = bf16[393216]{0:T(1024)(128)(2,1)} async-done(((bf16[393216]{0:T(1024)(128)(2,1)}), bf16[393216]{0:T(1024)(128)(2,1)}) %all-reduce.4.cloned.1.call-update) | async-done | bytes 786448 | tf_op jit(solution)/shard_map/psum | solution.py:28
  806.4 2.9 reshape.543
  809.3 3.6 copy.47
  812.9 3.1 convert_reduce_fusion
  816.8 1.5 add_add_fusion.3
  818.3 145.4 %all-reduce.6.cloned.1.call-done = (f32[8,2048,16]{1,2,0:T(8,128)}, f32[8,16,2048]{2,1,0:T(8,128)}, f32[8,2048,16]{1,2,0:T(8,128)}, f32[8,16,2048]{2,1,0:T(8,128)}) async-done(((f32[8,2048,16]{1,2,0:T(8,128)}, f32[8,16,2048]{2,1,0:T(8,128)}, f32[8,2048,16]{1,2,0:T(8,128)}, f32[8,16,2048]{2,1,0:T(8,128)}), (f32[8,2048,16]{1,2,0:T(8,128)}, f32[8,16,2048]{2,1,0:T(8,128)}, f32[8,2048,16]{1,2,0:T(8,128)}, ...) | async-done | bytes 4194320 | tf_op jit(solution)/shard_map/psum | solution.py:358
  963.7 2.4 copy.131
  966.1 2.3 copy.132
  (247 shorter events, 53.4 us)
Async XLA Ops:
  7.2 10.6 %copy-start = (bf16[8,2048,16]{1,2,0:T(8,128)(2,1)S(1)}, bf16[8,2048,16]{1,2,0:T(8,128)(2,1)}, u32[]{:S(2)}) copy-start(bf16[8,2048,16]{1,2,0:T(8,128)(2,1)} %param.42) | copy-start | bytes 1572868
  7.2 11.3 %copy-start.38 = (bf16[8,16,768]{2,1,0:T(8,128)(2,1)S(1)}, bf16[8,16,768]{2,1,0:T(8,128)(2,1)}, u32[]{:S(2)}) copy-start(bf16[8,16,768]{2,1,0:T(8,128)(2,1)} %param.43) | copy-start | bytes 589828
  7.2 11.5 %copy-start.24 = (bf16[8,16,2048]{2,1,0:T(8,128)(2,1)S(1)}, bf16[8,16,2048]{2,1,0:T(8,128)(2,1)}, u32[]{:S(2)}) copy-start(bf16[8,16,2048]{2,1,0:T(8,128)(2,1)} %param.45) | copy-start | bytes 1572868
  7.2 80.6 %all-gather.9.cloned.1.call-start = ((), (), s32[]{:S(2)}) async-start(), calls=%async_computation.4 | async-start | bytes 4718592 | tf_op jit(solution)/shard_map/all_gather | solution.py:200
  8.5 1.9 copy-start.43
  13.3 110.7 %all-gather.11.cloned.1.call-start = ((), (), s32[]{:S(2)}) async-start(), calls=%async_computation.5 | async-start | bytes 3342336 | tf_op jit(solution)/shard_map/all_gather | solution.py:202
  14.0 145.6 %all-gather.13.cloned.1.call-start = ((), (), s32[]{:S(2)}) async-start(), calls=%async_computation.6 | async-start | bytes 1114112 | tf_op jit(solution)/shard_map/all_gather | solution.py:203
  14.7 250.2 %all-gather.21.cloned.1.call-start = ((), (), s32[]{:S(2)}) async-start(), calls=%async_computation.10 | async-start | bytes 4718592 | tf_op jit(solution)/shard_map/all_gather | solution.py:267
  15.3 294.9 %all-gather.19.cloned.1.call-start = ((), (), s32[]{:S(2)}) async-start(), calls=%async_computation.9 | async-start | bytes 4456448 | tf_op jit(solution)/shard_map/all_gather | solution.py:243
  15.9 367.9 %all-gather.15.cloned.1.call-start = ((), (), s32[]{:S(2)}) async-start(), calls=%async_computation.7 | async-start | bytes 4718592 | tf_op jit(solution)/shard_map/all_gather | solution.py:240
  18.5 72.6 %copy-start.14 = (bf16[1,2048,16]{2,1,0:T(8,128)(2,1)}, bf16[1,2048,16]{2,1,0:T(8,128)(2,1)S(1)}, u32[]{:S(2)}) copy-start(bf16[1,2048,16]{2,1,0:T(8,128)(2,1)S(1)} %copy.49) | copy-start | bytes 196612
  18.7 111.6 %copy-start.36 = (bf16[1,16,768]{2,0,1:T(2,128)(2,1)}, bf16[1,16,768]{2,0,1:T(2,128)(2,1)S(1)}, u32[]{:S(2)}) copy-start(bf16[1,16,768]{2,0,1:T(2,128)(2,1)S(1)} %fusion.68) | copy-start | bytes 73732
  19.2 142.9 %copy-start.28 = (bf16[1,16,2048]{2,0,1:T(2,128)(2,1)}, bf16[1,16,2048]{2,0,1:T(2,128)(2,1)S(1)}, u32[]{:S(2)}) copy-start(bf16[1,16,2048]{2,0,1:T(2,128)(2,1)S(1)} %fusion.60) | copy-start | bytes 196612
  91.1 39.2 %copy-start.30 = (bf16[1024,16]{0,1:T(8,128)(2,1)}, bf16[1024,16]{0,1:T(8,128)(2,1)S(1)}, u32[]{:S(2)}) copy-start(bf16[1024,16]{0,1:T(8,128)(2,1)S(1)} %convolution_convert_fusion.5) | copy-start | bytes 98308
  91.1 39.2 %copy-start.50 = (f32[768]{0:T(1024)S(1)}, f32[768]{0:T(1024)}, u32[]{:S(2)}) copy-start(f32[768]{0:T(1024)} %param.33) | copy-start | bytes 9220
  153.3 8.8 copy-start.8
  153.9 8.2 copy-start.11
  154.2 8.0 copy-start.32
  225.6 1.0 copy-start.45
  225.6 1.6 copy-start.40
  225.6 1.6 copy-start.46
  226.7 2.4 copy-start.34
  226.7 2.8 copy-start.25
  226.7 3.6 copy-start.35
  228.3 193.3 %all-gather.17.cloned.1.call-start = ((), (), s32[]{:S(2)}) async-start(), calls=%async_computation.8 | async-start | bytes 4456448 | tf_op jit(solution)/shard_map/all_gather | solution.py:242
  387.2 42.3 %copy-start.56 = (f32[1024]{0:T(1024)S(1)}, f32[1024]{0:T(1024)}, u32[]{:S(2)}) copy-start(f32[1024]{0:T(1024)} %param.39) | copy-start | bytes 12292
  429.5 11.2 %copy-start.57 = (f32[1024,1024]{1,0:T(8,128)S(1)}, f32[1024,1024]{1,0:T(8,128)}, u32[]{:S(2)}) copy-start(f32[1024,1024]{1,0:T(8,128)} %fusion.100) | copy-start | bytes 12582916
  440.6 2.9 copy-start.55
  442.9 5.2 copy-start.13
  451.5 55.3 %all-to-all-start.2 = ((bf16[8,128,2048]{2,1,0:T(8,128)(2,1)}), bf16[8,128,2048]{2,1,0:T(8,128)(2,1)}, u32[]{:S(2)}, u32[]{:S(2)}) async-start(bf16[8,128,2048]{2,1,0:T(8,128)(2,1)} %bitcast.232), calls=%async_computation.2 | async-start | bytes 8388608 | tf_op jit(solution)/shard_map/all_to_all | solution.py:20
  506.8 53.8 %all-to-all-start.1 = ((bf16[8,128,2048]{2,1,0:T(8,128)(2,1)}), bf16[8,128,2048]{2,1,0:T(8,128)(2,1)}, u32[]{:S(2)}, u32[]{:S(2)}) async-start(bf16[8,128,2048]{2,1,0:T(8,128)(2,1)} %bitcast.231), calls=%async_computation.1 | async-start | bytes 8388608 | tf_op jit(solution)/shard_map/all_to_all | solution.py:20
  511.8 125.0 %all-gather.23.cloned.1.call-start = ((), (), s32[]{:S(2)}) async-start(), calls=%async_computation.11 | async-start | bytes 4718592 | tf_op jit(solution)/shard_map/all_gather | solution.py:298
  514.9 48.7 %copy-start.47 = (f32[2048]{0:T(1024)S(1)}, f32[2048]{0:T(1024)}, u32[]{:S(2)}) copy-start(f32[2048]{0:T(1024)} %param.41) | copy-start | bytes 24580
  560.6 5.2 copy-start.16
  564.8 2.1 copy-start.51
  566.8 233.7 %all-reduce.4.cloned.1.call-start = ((), (), s32[]{:S(2)}) async-start(), calls=%async_computation.12 | async-start | bytes 1572864 | tf_op jit(solution)/shard_map/psum | solution.py:28
  566.9 5.2 copy-start.41
  576.9 3.7 copy-start.2
  636.9 3.5 copy-start.12
  636.9 4.5 copy-start.5
  636.9 4.5 copy-start.18
  654.2 1.0 copy-start.7
  668.9 1.0 copy-start.7
  675.8 1.5 copy-start.29
  675.8 1.5 copy-start.42
  676.0 2.1 copy-start.21
  679.0 5.4 copy-start.15
  687.7 125.2 %all-to-all-start.3 = ((bf16[8,128,2048]{2,1,0:T(8,128)(2,1)}), bf16[8,128,2048]{2,1,0:T(8,128)(2,1)}, u32[]{:S(2)}, u32[]{:S(2)}) async-start(bf16[8,128,2048]{2,1,0:T(8,128)(2,1)} %bitcast.230), calls=%async_computation.3 | async-start | bytes 8388608 | tf_op jit(solution)/shard_map/all_to_all | solution.py:20
  692.3 3.1 copy-start.23
  692.3 4.7 copy-start.33
  692.3 271.4 %all-reduce.6.cloned.1.call-start = ((), (), s32[]{:S(2)}) async-start(), calls=%async_computation.13 | async-start | bytes 8388608 | tf_op jit(solution)/shard_map/psum | solution.py:358
  692.3 4.7 copy-start.6
  695.4 2.3 copy-start.22
  809.3 6.7 copy-start.4
  809.3 6.7 copy-start.39
  809.3 6.7 copy-start.44
  812.9 3.5 copy-start.54
  812.9 3.5 copy-start.49
  812.9 3.9 copy-start.10
  812.9 3.9 copy-start.17
  812.9 3.9 copy-start.52
  963.7 4.7 copy-start.20
  963.7 5.7 copy-start.19
  963.7 6.7 copy-start.1
  (10 other events, 9.0 us)
Sparse Core Ops, SparseCore 0:
  13.4 74.3 all-gather.8
  89.5 34.3 all-gather.10
  125.5 33.9 all-gather.12
  161.8 103.1 all-gather.20
  266.4 43.7 all-gather.18
  313.0 70.7 all-gather.14
  385.6 35.9 all-gather.16
  566.9 69.9 all-gather.22
  679.1 121.3 all-reduce.3
  807.4 156.1 all-reduce.5
where the time goes:
time: 982 us; the launch traced here: 978 us
  waiting for transfers between devices  666 us (68%)
  matrix products  139 us (14%)
  blocking collectives  62.2 us (6%)
  other arithmetic  40.9 us (4%)
  local copies, waits for them, and re-layouts  29.7 us (3%)
  starting transfers between devices  16.5 us (2%)
  between operations  16.2 us (2%)
    psum x1, waiting for transfers between devices, local(): lax.psum((spread(onehot_high, term_joined_in), spread(onehot_high, term_d...  145 us
    psum x1, waiting for transfers between devices, together(): so_far = lax.psum(jnp.concatenate([a.ravel() for a in arrays]), axis)  101 us
    all_to_all x3, waiting for transfers between devices, sum_at_owner(): lax.all_to_all(blocks, axis, split_axis=0, concat_axis=0, tiled=True)  81.6 us
    all_gather x1, waiting for transfers between devices, local(): gathered_one = lax.all_gather(normed_one, 'tp', axis=0, tiled=True)  68.6 us
    all_gather x1, waiting for transfers between devices, local(): gathered_two = lax.all_gather(normed_two, 'tp', axis=0, tiled=True)  63.6 us
    all_to_all x1, blocking collectives, sum_at_owner(): lax.all_to_all(blocks, axis, split_axis=0, concat_axis=0, tiled=True)  62.2 us
    all_gather x1, waiting for transfers between devices, local(): lax.all_gather(grad_mid.astype(jnp.bfloat16), 'tp', axis=0, tiled=True)  55 us
    all_gather x1, waiting for transfers between devices, local(): lax.all_gather(down_weight, 'fsdp', axis=1, tiled=True)  41.9 us
  transfers between devices with their start and end apart: 13, of which 12 were waited for; matrix products, arithmetic and copies ran while one was open for 13% of the time, Pallas kernels for 0%

commit v1 on v0

--- a/solution.py
+++ b/solution.py
@@ -355,15 +355,14 @@
             )
         )
     )
-    both_sums = lax.psum(
-        (
-            spread(onehot_high, term_joined_in),
-            spread(onehot_high, term_dense_out),
-            spread(onehot_high, term_up_in),
-            spread(onehot_high, term_down_out),
-        ),
-        ("fsdp", "tp"),
-    )
+    both_sums = (
+        spread(onehot_high, term_joined_in),
+        spread(onehot_high, term_dense_out),
+        spread(onehot_high, term_up_in),
+        spread(onehot_high, term_down_out),
+    )
+    for mesh_axis in ("tp", "fsdp"):
+        both_sums = lax.psum(both_sums, mesh_axis)
     return (
         layer_out,
         grad_tokens,

time: 982 us -> 1060 us (1.079)
  waiting for transfers between devices: 666 us -> 748 us
    psum x1 -> x2, waiting for transfers between devices: 145 us -> 229 us  [local(): both_sums = lax.psum(both_sums, mesh_axis)]
  transfers between devices with their start and end apart: 13 -> 14, of which waited for: 12 -> 13; matrix products, arithmetic and copies ran while one was open for 13% -> 12% of each run, Pallas kernels for 0% -> 0%
where the time goes in v1:
time: 1060 us
  waiting for transfers between devices  748 us (71%)
  matrix products  139 us (13%)
  blocking collectives  62.2 us (6%)
  other arithmetic  40.9 us (4%)
  local copies, waits for them, and re-layouts  28.5 us (3%)
  starting transfers between devices  16.8 us (2%)
  between operations  15.9 us (2%)
    psum x2, waiting for transfers between devices, local(): both_sums = lax.psum(both_sums, mesh_axis)  229 us
    psum x1, waiting for transfers between devices, together(): so_far = lax.psum(jnp.concatenate([a.ravel() for a in arrays]), axis)  100 us
    all_to_all x3, waiting for transfers between devices, sum_at_owner(): lax.all_to_all(blocks, axis, split_axis=0, concat_axis=0, tiled=True)  81.6 us
    all_gather x1, waiting for transfers between devices, local(): gathered_one = lax.all_gather(normed_one, 'tp', axis=0, tiled=True)  68.5 us
    all_gather x1, waiting for transfers between devices, local(): gathered_two = lax.all_gather(normed_two, 'tp', axis=0, tiled=True)  63.6 us
    all_to_all x1, blocking collectives, sum_at_owner(): lax.all_to_all(blocks, axis, split_axis=0, concat_axis=0, tiled=True)  62.2 us
    all_gather x1, waiting for transfers between devices, local(): lax.all_gather(grad_mid.astype(jnp.bfloat16), 'tp', axis=0, tiled=True)  55 us
    all_gather x1, waiting for transfers between devices, local(): lax.all_gather(down_weight, 'fsdp', axis=1, tiled=True)  41.9 us
  transfers between devices with their start and end apart: 14, of which 13 were waited for; matrix products, arithmetic and copies ran while one was open for 12% of the time, Pallas kernels for 0%

profile of v1, /device:TPU:1, one launch (start us, length us, event | category | flops | bytes accessed | tf_op | source)
XLA Modules:
  0.0 1058.3 jit_solution(17858091058051564245)
XLA Ops:
  9.9 2.3 fusion.50
  18.2 68.5 %all-gather.9.cloned.1.call-done = bf16[1024,2048]{1,0:T(8,128)(2,1)} async-done(((bf16[128,2048]{1,0:T(8,128)(2,1)}), bf16[1024,2048]{1,0:T(8,128)(2,1)}) %all-gather.9.cloned.1.call-update) | async-done | bytes 4194320 | tf_op jit(solution)/shard_map/all_gather | solution.py:200
  86.7 3.4 convolution_convert_fusion.5
  90.1 32.7 %all-gather.11.cloned.1.call-done = bf16[2048,768]{1,0:T(8,128)(2,1)} async-done(((bf16[128,768]{1,0:T(8,128)(2,1)}), bf16[2048,768]{1,0:T(8,128)(2,1)}) %all-gather.11.cloned.1.call-update) | async-done | bytes 3145744 | tf_op jit(solution)/shard_map/all_gather | solution.py:202
  122.9 6.4 fusion.96
  130.1 22.1 %while.28 = (s32[]{:T(128)}, bf16[2,512,4,64]{1,3,2,0:T(8,128)(2,1)S(1)}, f32[2,4,512]{2,1,0:T(4,128)S(1)}, s32[2]{0:T(128)S(1)}, bf16[1024,4,64]{0,2,1:T(8,128)...) while((s32[]{:T(128)}, ...), condition=%wide.region_5.6_spmd.clone, body=%wide.region_2.5_spmd.clone.sunk | while | flops 577370624 | bytes 37297388 | solution.py:104
  132.1 2.7 fusion.187
  134.8 2.9 fusion.188
  137.8 3.4 fusion.189
  143.2 2.7 fusion.187
  145.9 2.9 fusion.188
  148.8 3.4 fusion.189
  153.1 5.4 all-gather.13.cloned.1.call-done
  158.5 2.5 fusion.97
  162.4 62.2 %all_to_all.20 = bf16[8,128,2048]{2,1,0:T(8,128)(2,1)S(1)} all-to-all(bf16[8,128,2048]{2,1,0:T(8,128)(2,1)S(1)} %bitcast.233), channel_id=1, replica_groups=mesh['fsdp'=16,'tp'=8] {'tp'}, dimensions={0} | all-to-all | bytes 8388608 | tf_op jit(solution)/shard_map/all_to_all | solution.py:20
  229.5 1.5 fusion.56
  231.0 32.9 %all-gather.21.cloned.1.call-done = bf16[1024,2048]{1,0:T(8,128)(2,1)} async-done(((bf16[128,2048]{1,0:T(8,128)(2,1)}), bf16[1024,2048]{1,0:T(8,128)(2,1)}) %all-gather.21.cloned.1.call-update) | async-done | bytes 4194320 | tf_op jit(solution)/shard_map/all_gather | solution.py:267
  263.9 3.4 convolution_convert_fusion.3
  267.3 41.9 %all-gather.19.cloned.1.call-done = bf16[1024,2048]{1,0:T(8,128)(2,1)} async-done(((bf16[1024,128]{1,0:T(8,128)(2,1)}), bf16[1024,2048]{1,0:T(8,128)(2,1)}) %all-gather.19.cloned.1.call-update) | async-done | bytes 4194320 | tf_op jit(solution)/shard_map/all_gather | solution.py:243
  309.2 10.0 fusion.100
  319.2 63.6 %all-gather.15.cloned.1.call-done = bf16[1024,2048]{1,0:T(8,128)(2,1)} async-done(((bf16[128,2048]{1,0:T(8,128)(2,1)}), bf16[1024,2048]{1,0:T(8,128)(2,1)}) %all-gather.15.cloned.1.call-update) | async-done | bytes 4194320 | tf_op jit(solution)/shard_map/all_gather | solution.py:240
  382.8 3.4 convolution_convert_fusion.4
  386.2 34.3 %all-gather.17.cloned.1.call-done = bf16[2048,1024]{1,0:T(8,128)(2,1)} async-done(((bf16[128,1024]{1,0:T(8,128)(2,1)}), bf16[2048,1024]{1,0:T(8,128)(2,1)}) %all-gather.17.cloned.1.call-update) | async-done | bytes 4194320 | tf_op jit(solution)/shard_map/all_gather | solution.py:242
  420.5 8.0 fusion.98
  428.4 11.2 %multiply_convert_fusion.2 = (bf16[1024,1024]{1,0:T(8,128)(2,1)}, f32[1024,1024]{1,0:T(8,128)S(1)}, f32[1024,1024]{1,0:T(8,128)S(1)}) fusion(f32[1024]{0:T(1024)S(1)} %copy-done.56, f32[1024,1024]{1,0:T(8,128)S(1)} %fusion.98, bf16[1024,16]{0,1:T(8,128)(2,1)S(1)} %convolution_convert_fusion.4, bf16[1,16,1024]{2,0,1:T(2,128)(2,1)S(1)} %fusion.66), kind=kOutput, calls=%fused_computation.60 | convolution fusion | flops 103809024 | bytes 14749696 | tf_op jit(solution)/shard_map/slk,skn->sln/dot_general | solution.py:54
  439.6 2.3 add_convert_fusion.4
  442.6 4.6 fusion.101
  447.1 3.3 add_convert_fusion.1
  450.4 6.5 all-to-all-start.2
  457.0 2.2 convolution_convert_fusion.6
  459.2 6.9 fusion.99
  466.1 3.4 add_convert_fusion.2
  469.5 36.2 %all-to-all-done.2 = bf16[8,128,2048]{2,1,0:T(8,128)(2,1)} async-done(((bf16[8,128,2048]{2,1,0:T(8,128)(2,1)}), bf16[8,128,2048]{2,1,0:T(8,128)(2,1)}, u32[]{:S(2)}, u32[]{:S(2)}) %all-to-all-start.2) | async-done | bytes 4194336 | tf_op jit(solution)/shard_map/all_to_all | solution.py:20
  505.7 5.1 all-to-all-start.1
  510.8 3.0 convert_reduce_fusion.1
  514.2 45.4 %all-to-all-done.1 = bf16[8,128,2048]{2,1,0:T(8,128)(2,1)} async-done(((bf16[8,128,2048]{2,1,0:T(8,128)(2,1)}), bf16[8,128,2048]{2,1,0:T(8,128)(2,1)}, u32[]{:S(2)}, u32[]{:S(2)}) %all-to-all-start.1) | async-done | bytes 4194336 | tf_op jit(solution)/shard_map/all_to_all | solution.py:20
  559.5 3.0 convert_reduce_fusion.2
  565.9 2.0 fusion.106
  568.7 2.3 fusion.107
  571.1 1.8 multiply_convert_fusion.1
  572.8 3.0 reshape.539
  575.9 3.7 fusion.109
  580.9 55.0 %all-gather.23.cloned.1.call-done = bf16[1024,2048]{1,0:T(8,128)(2,1)} async-done(((bf16[128,2048]{1,0:T(8,128)(2,1)}), bf16[1024,2048]{1,0:T(8,128)(2,1)}) %all-gather.23.cloned.1.call-update) | async-done | bytes 4194320 | tf_op jit(solution)/shard_map/all_gather | solution.py:298
  635.9 3.5 convolution_convert_fusion.1
  642.7 29.7 %while.29 = (s32[]{:T(128)}, f32[1024,4,64]{0,2,1:T(8,128)S(1)}, f32[1024,4,64]{0,2,1:T(8,128)S(1)}, bf16[2,512,4,64]{1,3,2,0:T(8,128)(2,1)}, s32[2]{0:T(128)S(1...) while((s32[]{:T(128)}, f32[1024,4,64]{0,2,1:T(8,128)S(1)}, ...), condition=%wide.region_15.16_spmd.clone, body=%wide.region_13.15_spmd.clone.sunk | while | flops 1369307648 | bytes 81836928 | solution.py:142
  646.8 2.4 fusion.199
  649.2 3.9 multiply_reduce_fusion.4
  661.5 2.4 fusion.199
  663.9 3.9 multiply_reduce_fusion.4
  672.4 1.6 copy.42
  678.1 3.0 fusion.110
  681.1 1.6 broadcast_multiply_fusion.1
  683.4 1.6 broadcast_multiply_fusion
  685.0 5.4 fusion.103
  690.4 3.3 add_convert_fusion
  693.7 4.6 all-to-all-start.3
  698.4 100.2 %all-reduce.6.cloned.1.call-done = bf16[393216]{0:T(1024)(128)(2,1)} async-done(((bf16[393216]{0:T(1024)(128)(2,1)}), bf16[393216]{0:T(1024)(128)(2,1)}) %all-reduce.6.cloned.1.call-update) | async-done | bytes 786448 | tf_op jit(solution)/shard_map/psum | solution.py:28
  799.6 114.6 %all-reduce.10.cloned.1.call-done = (f32[8,2048,16]{1,2,0:T(8,128)}, f32[8,16,2048]{2,1,0:T(8,128)}, f32[8,2048,16]{1,2,0:T(8,128)}, f32[8,16,2048]{2,1,0:T(8,128)}) async-done(((f32[8,2048,16]{1,2,0:T(8,128)}, f32[8,16,2048]{2,1,0:T(8,128)}, f32[8,2048,16]{1,2,0:T(8,128)}, f32[8,16,2048]{2,1,0:T(8,128)}), (f32[8,2048,16]{1,2,0:T(8,128)}, f32[8,16,2048]{2,1,0:T(8,128)}, f32[8,2048,16]{1,2,0:T(8,128)}, ...) | async-done | bytes 4194320 | tf_op jit(solution)/shard_map/psum | solution.py:365
  919.1 2.7 reshape.543
  921.7 3.6 copy.47
  925.3 3.1 convert_reduce_fusion
  930.7 113.9 %all-reduce.8.cloned.1.call-done = (f32[8,2048,16]{1,2,0:T(8,128)}, f32[8,16,2048]{2,1,0:T(8,128)}, f32[8,2048,16]{1,2,0:T(8,128)}, f32[8,16,2048]{2,1,0:T(8,128)}) async-done(((f32[8,2048,16]{1,2,0:T(8,128)}, f32[8,16,2048]{2,1,0:T(8,128)}, f32[8,2048,16]{1,2,0:T(8,128)}, f32[8,16,2048]{2,1,0:T(8,128)}), (f32[8,2048,16]{1,2,0:T(8,128)}, f32[8,16,2048]{2,1,0:T(8,128)}, f32[8,2048,16]{1,2,0:T(8,128)}, ...) | async-done | bytes 4194320 | tf_op jit(solution)/shard_map/psum | solution.py:365
  1044.7 2.4 copy.135
  1047.1 2.3 copy.136
  (250 shorter events, 54.1 us)
Async XLA Ops:
  7.2 9.5 copy-start
  7.2 10.3 copy-start.38
  7.2 10.5 copy-start.24
  7.2 79.5 %all-gather.9.cloned.1.call-start = ((), (), s32[]{:S(2)}) async-start(), calls=%async_computation.4 | async-start | bytes 4718592 | tf_op jit(solution)/shard_map/all_gather | solution.py:200
  8.5 8.1 copy-start.43
  9.9 6.8 copy-start.53
  9.9 6.8 copy-start.48
  12.2 110.7 %all-gather.11.cloned.1.call-start = ((), (), s32[]{:S(2)}) async-start(), calls=%async_computation.5 | async-start | bytes 3342336 | tf_op jit(solution)/shard_map/all_gather | solution.py:202
  12.9 145.6 %all-gather.13.cloned.1.call-start = ((), (), s32[]{:S(2)}) async-start(), calls=%async_computation.6 | async-start | bytes 1114112 | tf_op jit(solution)/shard_map/all_gather | solution.py:203
  13.7 250.2 %all-gather.21.cloned.1.call-start = ((), (), s32[]{:S(2)}) async-start(), calls=%async_computation.10 | async-start | bytes 4718592 | tf_op jit(solution)/shard_map/all_gather | solution.py:267
  14.3 294.9 %all-gather.19.cloned.1.call-start = ((), (), s32[]{:S(2)}) async-start(), calls=%async_computation.9 | async-start | bytes 4456448 | tf_op jit(solution)/shard_map/all_gather | solution.py:243
  14.8 368.0 %all-gather.15.cloned.1.call-start = ((), (), s32[]{:S(2)}) async-start(), calls=%async_computation.7 | async-start | bytes 4718592 | tf_op jit(solution)/shard_map/all_gather | solution.py:240
  17.5 72.6 %copy-start.14 = (bf16[1,2048,16]{2,1,0:T(8,128)(2,1)}, bf16[1,2048,16]{2,1,0:T(8,128)(2,1)S(1)}, u32[]{:S(2)}) copy-start(bf16[1,2048,16]{2,1,0:T(8,128)(2,1)S(1)} %copy.49) | copy-start | bytes 196612
  17.7 111.6 %copy-start.36 = (bf16[1,16,768]{2,0,1:T(2,128)(2,1)}, bf16[1,16,768]{2,0,1:T(2,128)(2,1)S(1)}, u32[]{:S(2)}) copy-start(bf16[1,16,768]{2,0,1:T(2,128)(2,1)S(1)} %fusion.68) | copy-start | bytes 73732
  18.2 142.9 %copy-start.28 = (bf16[1,16,2048]{2,0,1:T(2,128)(2,1)}, bf16[1,16,2048]{2,0,1:T(2,128)(2,1)S(1)}, u32[]{:S(2)}) copy-start(bf16[1,16,2048]{2,0,1:T(2,128)(2,1)S(1)} %fusion.60) | copy-start | bytes 196612
  90.1 39.2 %copy-start.30 = (bf16[1024,16]{0,1:T(8,128)(2,1)}, bf16[1024,16]{0,1:T(8,128)(2,1)S(1)}, u32[]{:S(2)}) copy-start(bf16[1024,16]{0,1:T(8,128)(2,1)S(1)} %convolution_convert_fusion.5) | copy-start | bytes 98308
  90.1 39.2 %copy-start.50 = (f32[768]{0:T(1024)S(1)}, f32[768]{0:T(1024)}, u32[]{:S(2)}) copy-start(f32[768]{0:T(1024)} %param.33) | copy-start | bytes 9220
  152.2 8.8 copy-start.8
  152.9 8.2 copy-start.11
  153.1 8.0 copy-start.32
  224.6 1.6 copy-start.40
  224.6 1.6 copy-start.46
  225.6 2.4 copy-start.34
  225.6 2.8 copy-start.25
  225.6 3.6 copy-start.35
  227.2 193.2 %all-gather.17.cloned.1.call-start = ((), (), s32[]{:S(2)}) async-start(), calls=%async_computation.8 | async-start | bytes 4456448 | tf_op jit(solution)/shard_map/all_gather | solution.py:242
  386.2 42.3 %copy-start.56 = (f32[1024]{0:T(1024)S(1)}, f32[1024]{0:T(1024)}, u32[]{:S(2)}) copy-start(f32[1024]{0:T(1024)} %param.39) | copy-start | bytes 12292
  428.4 11.2 %copy-start.57 = (f32[1024,1024]{1,0:T(8,128)S(1)}, f32[1024,1024]{1,0:T(8,128)}, u32[]{:S(2)}) copy-start(f32[1024,1024]{1,0:T(8,128)} %fusion.100) | copy-start | bytes 12582916
  439.6 2.9 copy-start.55
  441.9 5.2 copy-start.13
  450.4 55.3 %all-to-all-start.2 = ((bf16[8,128,2048]{2,1,0:T(8,128)(2,1)}), bf16[8,128,2048]{2,1,0:T(8,128)(2,1)}, u32[]{:S(2)}, u32[]{:S(2)}) async-start(bf16[8,128,2048]{2,1,0:T(8,128)(2,1)} %bitcast.232), calls=%async_computation.2 | async-start | bytes 8388608 | tf_op jit(solution)/shard_map/all_to_all | solution.py:20
  505.7 53.8 %all-to-all-start.1 = ((bf16[8,128,2048]{2,1,0:T(8,128)(2,1)}), bf16[8,128,2048]{2,1,0:T(8,128)(2,1)}, u32[]{:S(2)}, u32[]{:S(2)}) async-start(bf16[8,128,2048]{2,1,0:T(8,128)(2,1)} %bitcast.231), calls=%async_computation.1 | async-start | bytes 8388608 | tf_op jit(solution)/shard_map/all_to_all | solution.py:20
  510.8 125.0 %all-gather.23.cloned.1.call-start = ((), (), s32[]{:S(2)}) async-start(), calls=%async_computation.11 | async-start | bytes 4718592 | tf_op jit(solution)/shard_map/all_gather | solution.py:298
  513.9 48.7 %copy-start.47 = (f32[2048]{0:T(1024)S(1)}, f32[2048]{0:T(1024)}, u32[]{:S(2)}) copy-start(f32[2048]{0:T(1024)} %param.41) | copy-start | bytes 24580
  559.5 5.2 copy-start.16
  563.8 2.1 copy-start.51
  565.8 232.8 %all-reduce.6.cloned.1.call-start = ((), (), s32[]{:S(2)}) async-start(), calls=%async_computation.12 | async-start | bytes 1572864 | tf_op jit(solution)/shard_map/psum | solution.py:28
  565.9 5.2 copy-start.41
  575.9 3.7 copy-start.2
  635.8 3.5 copy-start.12
  635.9 4.5 copy-start.5
  635.9 4.5 copy-start.18
  674.5 1.5 copy-start.29
  674.5 1.5 copy-start.42
  674.7 2.1 copy-start.21
  676.0 5.1 copy-start.23
  676.8 5.9 copy-start.33
  677.8 236.5 %all-reduce.10.cloned.1.call-start = ((), (), s32[]{:S(2)}) async-start(), calls=%async_computation.14 | async-start | bytes 8388608 | tf_op jit(solution)/shard_map/psum | solution.py:365
  678.1 4.6 copy-start.6
  681.1 2.3 copy-start.22
  685.0 5.4 copy-start.15
  693.7 231.6 %all-to-all-start.3 = ((bf16[8,128,2048]{2,1,0:T(8,128)(2,1)}), bf16[8,128,2048]{2,1,0:T(8,128)(2,1)}, u32[]{:S(2)}, u32[]{:S(2)}) async-start(bf16[8,128,2048]{2,1,0:T(8,128)(2,1)} %bitcast.230), calls=%async_computation.3 | async-start | bytes 8388608 | tf_op jit(solution)/shard_map/all_to_all | solution.py:20
  698.3 346.3 %all-reduce.8.cloned.1.call-start = ((), (), s32[]{:S(2)}) async-start(), calls=%async_computation.13 | async-start | bytes 8388608 | tf_op jit(solution)/shard_map/psum | solution.py:365
  921.7 6.7 copy-start.4
  921.7 6.7 copy-start.39
  921.7 6.7 copy-start.44
  925.3 3.5 copy-start.54
  925.3 3.5 copy-start.49
  925.3 3.9 copy-start.10
  925.3 3.9 copy-start.17
  925.3 3.9 copy-start.52
  1044.7 4.7 copy-start.20
  1044.7 5.7 copy-start.19
  1044.7 6.7 copy-start.1
  (11 other events, 11.0 us)
Sparse Core Ops, SparseCore 0:
  12.3 74.3 all-gather.8
  88.4 34.3 all-gather.10
  124.5 33.9 all-gather.12
  160.7 103.1 all-gather.20
  265.4 43.7 all-gather.18
  312.0 70.7 all-gather.14
  384.5 35.9 all-gather.16
  565.9 69.9 all-gather.22
  677.9 120.6 all-reduce.5
  801.9 112.2 all-reduce.9
  917.2 127.3 all-reduce.7
